TPU v7x, 32 devices: a whole 2x2x4 slice. The times are simulated.
32 devices in a mesh: req: 2 (over x), ctx: 4 (over y, core), tp: 4 (over z).
Axes of the slice: x: 2, y: 2, z: 4, core: 2. Of those that a mesh axis runs over, the one named last changes fastest.
Arguments:
- queries: bfloat16 [512, 16, 128], P('req', 'tp'), may hold values from -5 to 5
- new_keys: bfloat16 [512, 4, 128], P('req', 'tp'), may hold values from -5 to 5
- new_values: bfloat16 [512, 4, 128], P('req', 'tp'), may hold values from -24 to 24
- cache_keys: bfloat16 [2, 8192, 4, 128], P('req', 'ctx', 'tp'), may hold values from -5 to 5
- cache_values: bfloat16 [2, 8192, 4, 128], P('req', 'ctx', 'tp'), may hold values from -24 to 24
- cache_lengths: int32 [2], replicated, may hold values from 1 to 8192, as said below
- residual: bfloat16 [512, 2048], P(('req', 'ctx'), 'tp'), may hold values from -24 to 24
- out_weight: bfloat16 [2048, 2048], P('tp', 'ctx'), may hold values from -0.52734375 to 0.52734375
- norm_gain: float32 [2048], replicated, may hold values from 0.1 to 1.9
- expert_ids: int32 [512, 6], P(('req', 'ctx')), may hold values from 0 to 63, all different within a row; in each aligned block of 64 rows (0 to 63, 64 to 127, ...) at most 8 rows name the same one
- gate_weights: float32 [512, 6], P(('req', 'ctx')), may hold values from 0.1 to 1
- w_gate: bfloat16 [64, 2048, 1408], P('req', 'ctx', 'tp'), may hold values from -0.125 to 0.125
- w_up: bfloat16 [64, 2048, 1408], P('req', 'ctx', 'tp'), may hold values from -0.125 to 0.125
- w_down: bfloat16 [64, 1408, 2048], P('req', 'tp', 'ctx'), may hold values from -0.15625 to 0.15625
Outputs:
- layer_out: bfloat16 [512, 2048], P(('req', 'ctx'), 'tp')
Inputs may be any that keep to these rules, and one draw needn't show every extreme that they name: `cache_lengths`: the longest cached length equals 8192. `expert_ids`: within each aligned block of 64 tokens no expert is named by more than 8 routes, a bound that some block reaches.
All inputs are finite; a program needn't handle non-finite values.
Results may differ from a plain program's by a relative error of at most 0.006.
Values may be sent and summed in bfloat16 or wider, within the bound.
A program may use at most 384 MiB of HBM per device.

v0:
```python
import jax
import jax.numpy as jnp
from jax import lax
from jax.sharding import PartitionSpec as P

TOP = 6
CAP = 8
MASKED = -1e30


def attention_part(queries, new_keys, new_values, cache_keys, cache_values, length):
    ctx_pos, ctx_count = (lax.axis_index("ctx"), lax.axis_size("ctx"))
    tok_dev, heads, hd = queries.shape
    cache_dev = cache_keys.shape[1]
    block = tok_dev // ctx_count
    rows = heads * block
    q = queries.reshape(ctx_count, block, heads, hd).transpose(0, 2, 1, 3)
    q = q.reshape(ctx_count * rows, hd)
    keys = jnp.concatenate([cache_keys[0, :, 0, :], new_keys[:, 0, :]], 0)
    values = jnp.concatenate([cache_values[0, :, 0, :], new_values[:, 0, :]], 0)
    scores = jnp.dot(keys, q.T, preferred_element_type=jnp.float32) * hd ** (-0.5)
    key_at = jnp.arange(cache_dev + tok_dev, dtype=jnp.int32)[:, None]
    row_at = jnp.arange(ctx_count * rows, dtype=jnp.int32)[None, :]
    token = row_at // rows * block + row_at % block
    valid = jnp.where(
        key_at < cache_dev,
        ctx_pos * cache_dev + key_at < length,
        jnp.logical_and(ctx_pos == ctx_count - 1, key_at - cache_dev <= token),
    )
    scores = jnp.where(valid, scores, MASKED)
    top = jnp.max(scores, 0, keepdims=True)
    weights = jnp.where(valid, jnp.exp(scores - top), 0.0)
    total = jnp.sum(weights, 0, keepdims=True)
    sums = lax.dot_general(
        values,
        weights.astype(jnp.bfloat16),
        (((0,), (0,)), ((), ())),
        preferred_element_type=jnp.float32,
    )
    pack = jnp.concatenate([sums, top, total, jnp.zeros((6, ctx_count * rows), jnp.float32)], 0)
    return pack.reshape(hd + 8, ctx_count, rows).transpose(1, 0, 2)


def merge(packs, hd, heads):
    top = jnp.max(packs[:, hd : hd + 1], 0)
    factor = jnp.exp(packs[:, hd : hd + 1] - top)
    total = jnp.sum(factor * packs[:, hd + 1 : hd + 2], 0)
    out = (jnp.sum(factor * packs[:, :hd], 0) / total).astype(jnp.bfloat16)
    block = out.shape[1] // heads
    return out.reshape(hd, heads, block).transpose(2, 1, 0).reshape(block, heads * hd)


def route_tables(expert_ids, gate_weights, exp_dev):
    block = expert_ids.shape[0]
    both = jnp.concatenate([expert_ids.astype(jnp.float32), gate_weights], 1)
    both = lax.all_gather(both, ("req", "ctx"))
    blocks = both.shape[0]
    ids = both[:, :, :TOP].astype(jnp.int32)
    gates = both[:, :, TOP:]
    first = lax.axis_index("req") * exp_dev
    experts = first + jnp.arange(exp_dev, dtype=jnp.int32)
    hits = ids[:, :, :, None] == experts
    gate_at = jnp.sum(jnp.where(hits, gates[..., None], 0.0), 2)
    hit = jnp.any(hits, 2)
    earlier = jnp.tril(jnp.ones((block, block), jnp.bfloat16), -1)
    rank = jnp.einsum(
        "ij,bje->bie", earlier, hit.astype(jnp.bfloat16), preferred_element_type=jnp.float32
    )
    code = jnp.arange(blocks, dtype=jnp.int32)[:, None, None] * CAP + rank.astype(jnp.int32)
    code = jnp.where(hit, code, -1)
    flat = (blocks * block, exp_dev)
    return (code.reshape(flat).T, gate_at.reshape(flat).T)


def body(
    queries,
    new_keys,
    new_values,
    cache_keys,
    cache_values,
    cache_lengths,
    residual,
    out_weight,
    norm_gain,
    expert_ids,
    gate_weights,
    w_gate,
    w_up,
    w_down,
):
    ctx_pos, tp_pos, req_pos = (lax.axis_index(a) for a in ("ctx", "tp", "req"))
    ctx_count, req_count = (lax.axis_size("ctx"), lax.axis_size("req"))
    tok_dev, heads, hd = queries.shape
    block, share = residual.shape
    exp_dev = w_gate.shape[0]
    slots = req_count * ctx_count * CAP
    length = lax.dynamic_index_in_dim(cache_lengths, req_pos, 0, keepdims=False)
    code, gate_at = route_tables(expert_ids, gate_weights, exp_dev)
    swap = [
        (a * ctx_count + b, b * ctx_count + a) for a in range(ctx_count) for b in range(ctx_count)
    ]
    residual_t = lax.ppermute(residual, ("ctx", "tp"), swap)
    packs = attention_part(queries, new_keys, new_values, cache_keys, cache_values, length)
    packs = lax.all_to_all(packs, "ctx", 0, 0, tiled=True)
    attended = merge(packs, hd, heads)
    attended = lax.all_gather(attended, "ctx", tiled=True)
    part = jnp.dot(attended, out_weight, preferred_element_type=jnp.float32)
    part = part.reshape(-1, block, share)
    part = lax.all_to_all(part, "tp", 0, 0, tiled=True)
    hidden = jnp.sum(part, 0) + residual_t.astype(jnp.float32)
    squares = jnp.sum(hidden * hidden, 1)
    gain = lax.dynamic_slice_in_dim(norm_gain, ctx_pos * share, share, 0)
    scaled = (hidden * gain).astype(jnp.bfloat16)
    squares = lax.psum(squares, "ctx")
    factor = lax.rsqrt(squares / norm_gain.shape[0] + 1e-06)
    factor = lax.all_gather(factor, ("req", "tp"), tiled=True)
    scaled = lax.all_gather(scaled, ("req", "tp"), tiled=True)
    pick = code[:, None, :] == jnp.arange(slots, dtype=jnp.int32)[None, :, None]
    row_factor = jnp.sum(jnp.where(pick, factor, 0.0), -1, keepdims=True)
    row_gate = jnp.sum(jnp.where(pick, gate_at[:, None, :], 0.0), -1, keepdims=True)
    pick = pick.astype(jnp.bfloat16)
    rows = jnp.einsum("est,td->esd", pick, scaled, preferred_element_type=jnp.bfloat16)
    gate = jnp.einsum("esd,edf->esf", rows, w_gate, preferred_element_type=jnp.float32)
    up = jnp.einsum("esd,edf->esf", rows, w_up, preferred_element_type=jnp.float32)
    both = jnp.stack([gate, up], 2).astype(jnp.bfloat16)
    both = both.reshape(ctx_count, exp_dev * slots // ctx_count, 2, -1)
    both = lax.all_to_all(both, "ctx", 0, 0, tiled=True)
    both = both.astype(jnp.float32).sum(0)
    per = exp_dev * slots // ctx_count
    mine = lax.dynamic_slice_in_dim(row_factor.reshape(-1, 1), ctx_pos * per, per, 0)
    inner = (jax.nn.silu(both[:, 0] * mine) * (both[:, 1] * mine)).astype(jnp.bfloat16)
    inner = lax.all_gather(inner, "ctx", tiled=True).reshape(exp_dev, slots, -1)
    down = jnp.einsum("esf,efd->esd", inner, w_down, preferred_element_type=jnp.float32)
    down = (down * row_gate).astype(jnp.bfloat16)
    mixed = jnp.einsum("est,esd->td", pick, down, preferred_element_type=jnp.float32)
    mixed = mixed.astype(jnp.bfloat16).reshape(-1, block, share)
    mixed = lax.all_to_all(mixed, ("req", "tp"), 0, 0, tiled=True)
    out = hidden + jnp.sum(mixed.astype(jnp.float32), 0)
    return lax.ppermute(out.astype(jnp.bfloat16), ("ctx", "tp"), swap)


def solution(mesh):
    in_specs = (
        P("req", "tp", None),
        P("req", "tp", None),
        P("req", "tp", None),
        P("req", "ctx", "tp", None),
        P("req", "ctx", "tp", None),
        P(),
        P(("req", "ctx"), "tp"),
        P("tp", "ctx"),
        P(),
        P(("req", "ctx"), None),
        P(("req", "ctx"), None),
        P("req", "ctx", "tp"),
        P("req", "ctx", "tp"),
        P("req", "tp", "ctx"),
    )
    out_specs = P(("req", "ctx"), "tp")
    return jax.shard_map(body, mesh=mesh, in_specs=in_specs, out_specs=out_specs, check_vma=False)
```

profile of v0, /device:TPU:4, one launch (start us, length us, event | category | flops | bytes accessed | tf_op | source)
XLA Modules:
  0.0 254.7 jit_solution(7631431469196999747)
XLA Ops:
  6.6 1.0 copy.55
  7.6 1.2 dynamic_slice.10
  8.9 0.7 add_compare_fusion
  9.5 6.5 %fusion = (f32[1024]{0:T(1024)S(1)}, f32[2304,1024]{1,0:T(8,128)S(1)}) fusion(s32[1024]{0:T(1024)S(1)} %fusion.38, s32[2304]{0:T(1024)S(1)} %iota_add_fusion, pred[2304]{0:T(1024)(128)(4,1)S(1)} %get-tuple-element.17, pred[2304]{0:T(1024)(128)(4,1)S(1)} %get-tuple-element.18, pred[]{:T(512)S(6)} %eq.16, bf16[1024,128]{1,0:T(8,128)(2,1)S(1)} %bitcast.83, ...), kind=kOutput, calls=%fused_computation.3 | convolution fusion | flops 619314176 | bytes 10311169 | tf_op jit(solution)/shard_map/dot_general | solution.py:21
  16.0 0.0 copy-start.12
  16.0 0.0 copy-start.13
  16.0 4.7 %fusion.1 = f32[1024]{0:T(1024)S(1)} fusion(f32[2304,1024]{1,0:T(8,128)S(1)} %get-tuple-element.16, f32[1024]{0:T(1024)S(1)} %get-tuple-element.15, s32[1024]{0:T(1024)S(1)} %fusion.38, s32[2304]{0:T(1024)S(1)} %iota_add_fusion, pred[2304]{0:T(1024)(128)(4,1)S(1)} %get-tuple-element.17, pred[2304]{0:T(1024)(128)(4,1)S(1)} %get-tuple-element.18, pred[]{:T(512)S(6)} %eq.16), kind=kLoop, calls=%fused_computation.5 | loop fusion | flops 18873344 | bytes 9463297 | tf_op jit(solution)/shard_map/reduce_sum | solution.py:33
  20.8 0.0 copy-start.14
  20.8 0.0 copy-start.10
  20.8 0.0 copy-start.11
  20.8 4.0 %fusion.3 = f32[128,1024]{1,0:T(8,128)S(1)} fusion(f32[2304,1024]{1,0:T(8,128)S(1)} %get-tuple-element.16, f32[1024]{0:T(1024)S(1)} %get-tuple-element.15, s32[1024]{0:T(1024)S(1)} %fusion.38, s32[2304]{0:T(1024)S(1)} %iota_add_fusion, pred[2304]{0:T(1024)(128)(4,1)S(1)} %get-tuple-element.17, pred[2304]{0:T(1024)(128)(4,1)S(1)} %get-tuple-element.18, ...), kind=kOutput, calls=%fused_computation.7 | convolution fusion | flops 624033792 | bytes 10573313 | tf_op jit(solution)/shard_map/dot_general | solution.py:34
  24.9 0.1 pad.7.clone
  25.0 0.9 maximum_bitcast_fusion
  25.9 3.5 %all-to-all-start = ((f32[4,136,256]{2,1,0:T(8,128)}), f32[4,136,256]{2,1,0:T(8,128)S(1)}, u32[]{:S(2)}, u32[]{:S(2)}) async-start(f32[4,136,256]{2,1,0:T(8,128)} %maximum_bitcast_fusion), calls=%async_computation | async-start | bytes 1114112 | tf_op jit(solution)/shard_map/all_to_all | solution.py:104
  29.4 4.4 %collective-permute-start = (bf16[64,512]{1,0:T(8,128)(2,1)S(1)}, bf16[64,512]{1,0:T(8,128)(2,1)S(1)}, u32[]{:S(2)}, u32[]{:S(2)}) collective-permute-start(bf16[64,512]{1,0:T(8,128)(2,1)S(1)} %copy-done.14), channel_id=1, source_target_pairs={{0,0},{1,4},{2,8},{3,12},{4,1},{5,5},{6,9},{7,13},{8,2},{9,6},{10,... | collective-permute-start | bytes 196616 | tf_op jit(solution)/shard_map/ppermute | solution.py:102
  33.9 9.2 %all-gather.1 = f32[8,64,12]{1,2,0:T(8,128)S(1)} all-gather(f32[1,64,12]{1,2,0:T(8,128)S(1)} %maximum_bitcast_fusion.1), channel_id=2, replica_groups=mesh['req'=2,'ctx'=4,'tp'=4] {'req','ctx'}, dimensions={0}, use_global_device_ids=true | all-gather | bytes 27648 | tf_op jit(solution)/shard_map/all_gather | solution.py:56
  43.1 0.0 all-to-all-done
  43.2 0.1 copy.59
  43.3 0.1 div.31
  43.4 0.1 copy_bitcast_fusion.1
  43.5 5.8 %all_gather.18 = bf16[256,512]{1,0:T(8,128)(2,1)S(1)} all-gather(bf16[64,512]{1,0:T(8,128)(2,1)S(1)} %copy_bitcast_fusion.1), channel_id=1, replica_groups=mesh['req'=2,'ctx'=4,'tp'=4] {'ctx'}, dimensions={0}, use_global_device_ids=true | all-gather | bytes 327680 | tf_op jit(solution)/shard_map/all_gather | solution.py:106
  49.4 1.1 fusion.53
  50.5 5.1 %all-to-all-start.1 = ((f32[4,64,512]{2,1,0:T(8,128)}), f32[4,64,512]{2,1,0:T(8,128)S(1)}, u32[]{:S(2)}, u32[]{:S(2)}) async-start(f32[4,64,512]{2,1,0:T(8,128)} %bitcast.13), calls=%async_computation.1 | async-start | bytes 1048576 | tf_op jit(solution)/shard_map/all_to_all | solution.py:109
  55.6 0.6 fusion.52
  56.2 0.6 copy-done.2
  56.8 0.2 compare_reduce_fusion
  57.0 0.2 fusion.13
  57.2 0.1 copy.61
  57.3 0.1 reshape.144
  57.4 0.8 dynamic_slice.11
  58.2 12.4 %all-to-all-done.1 = f32[4,64,512]{2,1,0:T(8,128)S(1)} async-done(((f32[4,64,512]{2,1,0:T(8,128)}), f32[4,64,512]{2,1,0:T(8,128)S(1)}, u32[]{:S(2)}, u32[]{:S(2)}) %all-to-all-start.1) | async-done | bytes 524320 | tf_op jit(solution)/shard_map/all_to_all | solution.py:109
  70.7 0.0 collective-permute-done
  70.7 0.1 multiply_reduce_fusion
  70.8 32.5 %all_gather.21 = bf16[512,512]{1,0:T(8,128)(2,1)S(1)} all-gather(bf16[64,512]{1,0:T(8,128)(2,1)S(1)} %get-tuple-element.12), channel_id=1, replica_groups=mesh['req'=2,'ctx'=4,'tp'=4] {'req','tp'}, dimensions={0}, use_global_device_ids=true | all-gather | bytes 589824 | tf_op jit(solution)/shard_map/all_gather | solution.py:117
  103.3 1.3 fusion.6
  104.6 8.6 %convolution_convert_fusion = bf16[32,64,352]{2,1,0:T(8,128)(2,1)} fusion(bf16[32,64,512]{2,1,0:T(8,128)(2,1)S(1)} %fusion.6, bf16[32,512,352]{1,2,0:T(8,128)(2,1)} %param.26), kind=kOutput, calls=%fused_computation.17 | convolution fusion | flops 738918400 | bytes 15073280 | tf_op jit(solution)/shard_map/esd,edf->esf/dot_general | solution.py:124
  113.2 2.5 copy.63
  115.7 8.6 %convolution_convert_fusion.1 = bf16[32,64,352]{2,1,0:T(8,128)(2,1)} fusion(bf16[32,64,512]{2,1,0:T(8,128)(2,1)S(1)} %fusion.6, bf16[32,512,352]{1,2,0:T(8,128)(2,1)} %param.25), kind=kOutput, calls=%fused_computation.18 | convolution fusion | flops 738918400 | bytes 15073280 | tf_op jit(solution)/shard_map/esd,edf->esf/dot_general | solution.py:123
  124.3 1.7 copy.62
  126.0 3.2 %pad_maximum_fusion = bf16[4,512,2,352]{1,3,2,0:T(8,128)(2,1)} fusion(bf16[4,512,1,352]{1,3,2,0:T(8,128)(2,1)} %copy.63, bf16[4,512,1,352]{1,3,2,0:T(8,128)(2,1)S(1)} %copy.62), kind=kLoop, calls=%fused_computation.14 | loop fusion | flops 1441792 | bytes 5767168 | tf_op jit(solution)/shard_map/stack | solution.py:125
  129.3 5.4 %all-to-all-start.2 = ((bf16[4,512,2,352]{1,3,2,0:T(8,128)(2,1)}), bf16[4,512,2,352]{1,3,2,0:T(8,128)(2,1)S(1)}, u32[]{:S(2)}, u32[]{:S(2)}) async-start(bf16[4,512,2,352]{1,3,2,0:T(8,128)(2,1)} %pad_maximum_fusion), calls=%async_computation.2 | async-start | bytes 5767168 | tf_op jit(solution)/shard_map/all_to_all | solution.py:127
  134.6 0.2 fusion.14
  134.8 0.1 copy.67
  134.9 0.1 reshape.146
  135.0 0.6 dynamic-slice
  136.3 33.5 %psum.7 = f32[64]{0:T(128)S(1)} all-reduce(f32[64]{0:T(128)S(1)} %get-tuple-element.11), channel_id=1, replica_groups=mesh['req'=2,'ctx'=4,'tp'=4] {'ctx'}, use_global_device_ids=true, to_apply=%region_9.10 | all-reduce | flops 64 | bytes 512 | tf_op jit(solution)/shard_map/psum | solution.py:114
  169.8 0.1 rsqrt_dynamic-update-slice_fusion
  169.9 18.9 %all-reduce = f32[512]{0:T(512)S(1)} all-reduce(f32[512]{0:T(512)S(1)} %rsqrt_dynamic-update-slice_fusion), channel_id=1, replica_groups=mesh['req'=2,'ctx'=4,'tp'=4] {'req','tp'}, use_global_device_ids=true, to_apply=%add | all-reduce | flops 512 | bytes 4096
  188.8 1.5 select_reduce_fusion
  190.3 0.1 reshape_broadcast_in_dim.3
  190.4 0.4 convert_reduce_fusion
  190.8 0.0 copy-start.6
  190.8 0.1 fusion.51
  190.9 0.3 copy.73
  191.2 0.3 copy.72
  191.5 1.0 fusion.16
  192.5 0.0 all-gather.4.cloned.1.call-update
  192.5 17.0 %all-gather.4.cloned.1.call-done = bf16[2048,352]{1,0:T(8,128)(2,1)} async-done(((bf16[512,352]{1,0:T(8,128)(2,1)}), bf16[2048,352]{1,0:T(8,128)(2,1)}) %all-gather.4.cloned.1.call-update) | async-done | bytes 1441808 | tf_op jit(solution)/shard_map/all_gather | solution.py:132
  209.5 8.2 %fusion.10 = bf16[512,512]{1,0:T(8,128)(2,1)S(1)} fusion(s32[32,512]{1,0:T(8,128)S(1)} %bitcast.86, bf16[32,64,352]{2,1,0:T(8,128)(2,1)} %bitcast.92, bf16[32,352,512]{2,1,0:T(8,128)(2,1)} %param.27, f32[32,64]{1,0:T(8,128)S(1)} %get-tuple-element.5), kind=kOutput, calls=%fused_computation.20 | convolution fusion | flops 1815347200 | bytes 13574144 | tf_op jit(solution)/shard_map/est,esd->td/dot_general | solution.py:135
  217.8 21.4 %all_to_all.20 = bf16[8,64,512]{2,1,0:T(8,128)(2,1)S(1)} all-to-all(bf16[8,64,512]{2,1,0:T(8,128)(2,1)S(1)} %bitcast.81), channel_id=1, replica_groups=mesh['req'=2,'ctx'=4,'tp'=4] {'req','tp'}, dimensions={0} | all-to-all | bytes 1048576 | tf_op jit(solution)/shard_map/all_to_all | solution.py:137
  239.1 0.1 convert_reduce_fusion.1
  239.2 2.7 %collective-permute-start.1 = (bf16[64,512]{1,0:T(8,128)(2,1)S(1)}, bf16[64,512]{1,0:T(8,128)(2,1)S(1)}, u32[]{:S(2)}, u32[]{:S(2)}) collective-permute-start(bf16[64,512]{1,0:T(8,128)(2,1)S(1)} %add_convert_fusion), channel_id=1, source_target_pairs={{0,0},{1,4},{2,8},{3,12},{4,1},{5,5},{6,9},{7,13},{8,2},{9,6},{10,... | collective-permute-start | bytes 196616 | tf_op jit(solution)/shard_map/ppermute | solution.py:139
  242.0 5.2 %collective-permute-done.1 = bf16[64,512]{1,0:T(8,128)(2,1)S(1)} collective-permute-done((bf16[64,512]{1,0:T(8,128)(2,1)S(1)}, bf16[64,512]{1,0:T(8,128)(2,1)S(1)}, u32[]{:S(2)}, u32[]{:S(2)}) %collective-permute-start.1) | collective-permute-done | bytes 65568 | tf_op jit(solution)/shard_map/ppermute | solution.py:139
  247.2 0.6 copy.83
  (45 shorter events, 0.3 us)
Async XLA Ops:
  6.5 42.9 %copy-start = (bf16[512,512]{1,0:T(8,128)(2,1)S(1)}, bf16[512,512]{1,0:T(8,128)(2,1)}, u32[]{:S(2)}) copy-start(bf16[512,512]{1,0:T(8,128)(2,1)} %param.21) | copy-start | bytes 1572868
  16.0 4.8 %copy-start.12 = (bf16[1,2048,1,128]{3,1,2,0:T(8,128)(2,1)S(1)}, bf16[1,2048,1,128]{3,1,2,0:T(8,128)(2,1)}, u32[]{:S(2)}) copy-start(bf16[1,2048,1,128]{3,1,2,0:T(8,128)(2,1)} %param.18) | copy-start | bytes 1572868
  16.0 4.8 %copy-start.13 = (bf16[256,1,128]{2,0,1:T(8,128)(2,1)S(1)}, bf16[256,1,128]{2,0,1:T(8,128)(2,1)}, u32[]{:S(2)}) copy-start(bf16[256,1,128]{2,0,1:T(8,128)(2,1)} %param.16) | copy-start | bytes 196612
  20.8 8.6 %copy-start.14 = (bf16[64,512]{1,0:T(8,128)(2,1)S(1)}, bf16[64,512]{1,0:T(8,128)(2,1)}, u32[]{:S(2)}) copy-start(bf16[64,512]{1,0:T(8,128)(2,1)} %param.20) | copy-start | bytes 196612
  20.8 13.0 %copy-start.10 = (s32[64,6]{0,1:T(8,128)S(1)}, s32[64,6]{0,1:T(8,128)}, u32[]{:S(2)}) copy-start(s32[64,6]{0,1:T(8,128)} %param.23) | copy-start | bytes 4612
  20.8 13.1 %copy-start.11 = (f32[64,6]{0,1:T(8,128)S(1)}, f32[64,6]{0,1:T(8,128)}, u32[]{:S(2)}) copy-start(f32[64,6]{0,1:T(8,128)} %param.24) | copy-start | bytes 4612
  25.9 17.2 %all-to-all-start = ((f32[4,136,256]{2,1,0:T(8,128)}), f32[4,136,256]{2,1,0:T(8,128)S(1)}, u32[]{:S(2)}, u32[]{:S(2)}) async-start(f32[4,136,256]{2,1,0:T(8,128)} %maximum_bitcast_fusion), calls=%async_computation | async-start | bytes 1114112 | tf_op jit(solution)/shard_map/all_to_all | solution.py:104
  29.4 41.3 %collective-permute-start = (bf16[64,512]{1,0:T(8,128)(2,1)S(1)}, bf16[64,512]{1,0:T(8,128)(2,1)S(1)}, u32[]{:S(2)}, u32[]{:S(2)}) collective-permute-start(bf16[64,512]{1,0:T(8,128)(2,1)S(1)} %copy-done.14), channel_id=1, source_target_pairs={{0,0},{1,4},{2,8},{3,12},{4,1},{5,5},{6,9},{7,13},{8,2},{9,6},{10,... | collective-permute-start | bytes 196616 | tf_op jit(solution)/shard_map/ppermute | solution.py:102
  50.5 20.1 %all-to-all-start.1 = ((f32[4,64,512]{2,1,0:T(8,128)}), f32[4,64,512]{2,1,0:T(8,128)S(1)}, u32[]{:S(2)}, u32[]{:S(2)}) async-start(f32[4,64,512]{2,1,0:T(8,128)} %bitcast.13), calls=%async_computation.1 | async-start | bytes 1048576 | tf_op jit(solution)/shard_map/all_to_all | solution.py:109
  56.2 0.6 copy-start.2
  57.4 55.8 %copy-start.4 = (s32[512,32]{0,1:T(8,128)}, s32[512,32]{0,1:T(8,128)S(1)}, u32[]{:S(2)}) copy-start(s32[512,32]{0,1:T(8,128)S(1)} %reshape.144) | copy-start | bytes 196612
  70.7 42.5 %copy-start.7 = (bf16[64,512]{1,0:T(8,128)(2,1)}, bf16[64,512]{1,0:T(8,128)(2,1)S(1)}, u32[]{:S(2)}) copy-start(bf16[64,512]{1,0:T(8,128)(2,1)S(1)} %collective-permute-done) | copy-start | bytes 196612
  129.2 5.4 %copy-start.3 = (s32[8,64,6]{1,2,0:T(8,128)S(1)}, s32[8,64,6]{1,2,0:T(8,128)}, u32[]{:S(2)}) copy-start(s32[8,64,6]{1,2,0:T(8,128)} %copy-done.2) | copy-start | bytes 36868
  129.2 5.4 %copy-start.9 = (f32[8,64,6]{1,2,0:T(8,128)S(1)}, f32[8,64,6]{1,2,0:T(8,128)}, u32[]{:S(2)}) copy-start(f32[8,64,6]{1,2,0:T(8,128)} %get-tuple-element.13) | copy-start | bytes 36868
  129.3 5.7 %copy-start.15 = (u32[32]{0:T(128)S(1)}, u32[32]{0:T(128)}, u32[]{:S(2)}) copy-start(u32[32]{0:T(128)} %constant.96) | copy-start | bytes 388
  129.3 59.5 %copy-start.5 = (s32[512,32]{0,1:T(8,128)S(1)}, s32[512,32]{0,1:T(8,128)}, u32[]{:S(2)}) copy-start(s32[512,32]{0,1:T(8,128)} %copy-done.4) | copy-start | bytes 196612
  129.3 61.1 %all-to-all-start.2 = ((bf16[4,512,2,352]{1,3,2,0:T(8,128)(2,1)}), bf16[4,512,2,352]{1,3,2,0:T(8,128)(2,1)S(1)}, u32[]{:S(2)}, u32[]{:S(2)}) async-start(bf16[4,512,2,352]{1,3,2,0:T(8,128)(2,1)} %pad_maximum_fusion), calls=%async_computation.2 | async-start | bytes 5767168 | tf_op jit(solution)/shard_map/all_to_all | solution.py:127
  134.6 74.9 %all-gather.4.cloned.1.call-start = ((), (), s32[]{:S(2)}) async-start(), calls=%async_computation.4 | async-start | bytes 1966080 | tf_op jit(solution)/shard_map/all_gather | solution.py:132
  190.8 18.7 %copy-start.6 = (s32[512,32]{0,1:T(8,128)S(1)}, s32[512,32]{0,1:T(8,128)}, u32[]{:S(2)}) copy-start(s32[512,32]{0,1:T(8,128)} %copy-done.4) | copy-start | bytes 196612
  209.5 29.7 %copy-start.8 = (bf16[64,512]{1,0:T(8,128)(2,1)S(1)}, bf16[64,512]{1,0:T(8,128)(2,1)}, u32[]{:S(2)}) copy-start(bf16[64,512]{1,0:T(8,128)(2,1)} %copy-done.7) | copy-start | bytes 196612
  209.5 38.4 %copy-start.1 = (bf16[512,512]{1,0:T(8,128)(2,1)S(1)}, bf16[512,512]{1,0:T(8,128)(2,1)}, u32[]{:S(2)}) copy-start(bf16[512,512]{1,0:T(8,128)(2,1)} %param.21) | copy-start | bytes 1572868
  239.2 8.0 %collective-permute-start.1 = (bf16[64,512]{1,0:T(8,128)(2,1)S(1)}, bf16[64,512]{1,0:T(8,128)(2,1)S(1)}, u32[]{:S(2)}, u32[]{:S(2)}) collective-permute-start(bf16[64,512]{1,0:T(8,128)(2,1)S(1)} %add_convert_fusion), channel_id=1, source_target_pairs={{0,0},{1,4},{2,8},{3,12},{4,1},{5,5},{6,9},{7,13},{8,2},{9,6},{10,... | collective-permute-start | bytes 196616 | tf_op jit(solution)/shard_map/ppermute | solution.py:139
Sparse Core Ops, SparseCore 0:
  192.7 16.7 all-gather.3
where the time goes:
time: 256 us; the launch traced here: 255 us
  blocking collectives  121 us (47%)
  matrix products  38.5 us (15%)
  waiting for transfers between devices  34.6 us (14%)
  starting transfers between devices  21.2 us (8%)
  between operations  14.5 us (6%)
  other arithmetic  14 us (5%)
  local copies, waits for them, and re-layouts  10.6 us (4%)
    psum x1, blocking collectives, body(): squares = lax.psum(squares, 'ctx')  33.5 us
    all_gather x1, blocking collectives, body(): scaled = lax.all_gather(scaled, ('req', 'tp'), tiled=True)  32.5 us
    all_to_all x1, blocking collectives, body(): mixed = lax.all_to_all(mixed, ('req', 'tp'), 0, 0, tiled=True)  21.4 us
    unnamed x1, blocking collectives  18.9 us
    all_gather x1, waiting for transfers between devices, body(): inner = lax.all_gather(inner, 'ctx', tiled=True).reshape(exp_dev, slots, -1)  17 us
    all_to_all x1, waiting for transfers between devices, body(): part = lax.all_to_all(part, 'tp', 0, 0, tiled=True)  12.4 us
    all_gather x1, blocking collectives, route_tables(): both = lax.all_gather(both, ('req', 'ctx'))  9.25 us
    dot_general x1, matrix products, body(): jnp.einsum('esd,edf->esf', rows, w_up, preferred_element_type=jnp.float32)  8.61 us
  transfers between devices with their start and end apart: 6, of which 3 were waited for; matrix products, arithmetic and copies ran while one was open for 2% of the time, Pallas kernels for 0%

commit v1 on v0

--- a/solution.py
+++ b/solution.py
@@ -114,7 +114,27 @@
     squares = lax.psum(squares, "ctx")
     factor = lax.rsqrt(squares / norm_gain.shape[0] + 1e-06)
     factor = lax.all_gather(factor, ("req", "tp"), tiled=True)
-    scaled = lax.all_gather(scaled, ("req", "tp"), tiled=True)
+    ways, here, step = (
+        lax.axis_size(("req", "tp")),
+        lax.axis_index(("req", "tp")),
+        scaled.shape[0],
+    )
+    shape = [n * ways if d == 0 else n for d, n in enumerate(scaled.shape)]
+    full = lax.dynamic_update_slice_in_dim(
+        jnp.zeros(shape, scaled.dtype), scaled, here * step, axis=0
+    )
+    going_up = going_down = scaled
+    for far in range(1, ways // 2 + 1):
+        going_up = lax.ppermute(going_up, ("req", "tp"), [(d, (d + 1) % ways) for d in range(ways)])
+        full = lax.dynamic_update_slice_in_dim(full, going_up, (here - far) % ways * step, axis=0)
+        if 2 * far < ways:
+            going_down = lax.ppermute(
+                going_down, ("req", "tp"), [(d, (d - 1) % ways) for d in range(ways)]
+            )
+            full = lax.dynamic_update_slice_in_dim(
+                full, going_down, (here + far) % ways * step, axis=0
+            )
+    scaled = full
     pick = code[:, None, :] == jnp.arange(slots, dtype=jnp.int32)[None, :, None]
     row_factor = jnp.sum(jnp.where(pick, factor, 0.0), -1, keepdims=True)
     row_gate = jnp.sum(jnp.where(pick, gate_at[:, None, :], 0.0), -1, keepdims=True)

time: 256 us -> 246 us (0.961)
  blocking collectives: 121 us -> 87.2 us
  starting transfers between devices: 21.2 us -> 38.2 us
  waiting for transfers between devices: 34.6 us -> 42.2 us
    all_gather x1 -> x0, blocking collectives: 32.5 us -> none  [body(): scaled = lax.all_gather(scaled, ('req', 'tp'), tiled=True)]
    ppermute x0 -> x7, starting transfers between devices: none -> 15.3 us  [the longest x3 15.2 us: body(): lax.ppermute(going_down, ('req', 'tp'), [(d, (d - 1) % ways) for d in ran...]
    ppermute x0 -> x7, waiting for transfers between devices: none -> 12.1 us  [the longest x4 11.4 us: body(): lax.ppermute(going_up, ('req', 'tp'), [(d, (d + 1) % ways) for d in range...]
    all_to_all x1, waiting for transfers between devices: 12.4 us -> 4.51 us  [body(): part = lax.all_to_all(part, 'tp', 0, 0, tiled=True)]
  transfers between devices with their start and end apart: 6 -> 13, of which waited for: 3 -> 11; matrix products, arithmetic and copies ran while one was open for 2% -> 3% of each run, Pallas kernels for 0% -> 0%
where the time goes in v1:
time: 246 us; the launch traced here: 245 us
  blocking collectives  87.2 us (35%)
  waiting for transfers between devices  42.2 us (17%)
  matrix products  38.5 us (16%)
  starting transfers between devices  38.2 us (16%)
  between operations  14.7 us (6%)
  other arithmetic  14 us (6%)
  local copies, waits for them, and re-layouts  10.5 us (4%)
    psum x1, blocking collectives, body(): squares = lax.psum(squares, 'ctx')  33.4 us
    all_to_all x1, blocking collectives, body(): mixed = lax.all_to_all(mixed, ('req', 'tp'), 0, 0, tiled=True)  21.3 us
    all_gather x1, waiting for transfers between devices, body(): inner = lax.all_gather(inner, 'ctx', tiled=True).reshape(exp_dev, slots, -1)  18.3 us
    unnamed x1, blocking collectives  17.4 us
    ppermute x3, starting transfers between devices, body(): lax.ppermute(going_down, ('req', 'tp'), [(d, (d - 1) % ways) for d in ran...  15.2 us
    ppermute x4, waiting for transfers between devices, body(): lax.ppermute(going_up, ('req', 'tp'), [(d, (d + 1) % ways) for d in range...  11.4 us
    all_gather x1, blocking collectives, route_tables(): both = lax.all_gather(both, ('req', 'ctx'))  9.25 us
    dot_general x1, matrix products, body(): jnp.einsum('esd,edf->esf', rows, w_gate, preferred_element_type=jnp.float32)  8.61 us
  transfers between devices with their start and end apart: 13, of which 11 were waited for; matrix products, arithmetic and copies ran while one was open for 3% of the time, Pallas kernels for 0%

profile of v1, /device:TPU:4, one launch (start us, length us, event | category | flops | bytes accessed | tf_op | source)
XLA Modules:
  0.0 245.4 jit_solution(7524411711137591661)
XLA Ops:
  6.6 1.0 copy.55
  7.6 1.2 dynamic_slice.10
  8.9 0.7 add_compare_fusion
  9.5 6.5 %fusion = (f32[1024]{0:T(1024)S(1)}, f32[2304,1024]{1,0:T(8,128)S(1)}) fusion(s32[1024]{0:T(1024)S(1)} %fusion.38, s32[2304]{0:T(1024)S(1)} %iota_add_fusion, pred[2304]{0:T(1024)(128)(4,1)S(1)} %get-tuple-element.17, pred[2304]{0:T(1024)(128)(4,1)S(1)} %get-tuple-element.18, pred[]{:T(512)S(6)} %eq.39, bf16[1024,128]{1,0:T(8,128)(2,1)S(1)} %bitcast.83, ...), kind=kOutput, calls=%fused_computation.3 | convolution fusion | flops 619314176 | bytes 10311169 | tf_op jit(solution)/shard_map/dot_general | solution.py:21
  16.0 4.7 %fusion.1 = f32[1024]{0:T(1024)S(1)} fusion(f32[2304,1024]{1,0:T(8,128)S(1)} %get-tuple-element.16, f32[1024]{0:T(1024)S(1)} %get-tuple-element.15, s32[1024]{0:T(1024)S(1)} %fusion.38, s32[2304]{0:T(1024)S(1)} %iota_add_fusion, pred[2304]{0:T(1024)(128)(4,1)S(1)} %get-tuple-element.17, pred[2304]{0:T(1024)(128)(4,1)S(1)} %get-tuple-element.18, pred[]{:T(512)S(6)} %eq.39), kind=kLoop, calls=%fused_computation.5 | loop fusion | flops 18873344 | bytes 9463297 | tf_op jit(solution)/shard_map/reduce_sum | solution.py:33
  20.8 4.0 %fusion.3 = f32[128,1024]{1,0:T(8,128)S(1)} fusion(f32[2304,1024]{1,0:T(8,128)S(1)} %get-tuple-element.16, f32[1024]{0:T(1024)S(1)} %get-tuple-element.15, s32[1024]{0:T(1024)S(1)} %fusion.38, s32[2304]{0:T(1024)S(1)} %iota_add_fusion, pred[2304]{0:T(1024)(128)(4,1)S(1)} %get-tuple-element.17, pred[2304]{0:T(1024)(128)(4,1)S(1)} %get-tuple-element.18, ...), kind=kOutput, calls=%fused_computation.7 | convolution fusion | flops 624033792 | bytes 10573313 | tf_op jit(solution)/shard_map/dot_general | solution.py:34
  24.9 0.1 pad.7.clone
  25.0 0.9 maximum_bitcast_fusion
  25.9 3.5 %all-to-all-start = ((f32[4,136,256]{2,1,0:T(8,128)}), f32[4,136,256]{2,1,0:T(8,128)S(1)}, u32[]{:S(2)}, u32[]{:S(2)}) async-start(f32[4,136,256]{2,1,0:T(8,128)} %maximum_bitcast_fusion), calls=%async_computation | async-start | bytes 1114112 | tf_op jit(solution)/shard_map/all_to_all | solution.py:104
  29.4 4.5 %collective-permute-start = (bf16[64,512]{1,0:T(8,128)(2,1)S(1)}, bf16[64,512]{1,0:T(8,128)(2,1)S(1)}, u32[]{:S(2)}, u32[]{:S(2)}) collective-permute-start(bf16[64,512]{1,0:T(8,128)(2,1)S(1)} %copy-done.15), channel_id=1, source_target_pairs={{0,0},{1,4},{2,8},{3,12},{4,1},{5,5},{6,9},{7,13},{8,2},{9,6},{10,... | collective-permute-start | bytes 196616 | tf_op jit(solution)/shard_map/ppermute | solution.py:102
  33.9 0.8 dynamic_slice.11
  34.6 2.2 all-to-all-done
  36.9 0.1 copy.59
  37.0 0.1 div.31
  37.1 0.1 copy_bitcast_fusion.1
  37.2 5.8 %all_gather.15 = bf16[256,512]{1,0:T(8,128)(2,1)S(1)} all-gather(bf16[64,512]{1,0:T(8,128)(2,1)S(1)} %copy_bitcast_fusion.1), channel_id=1, replica_groups=mesh['req'=2,'ctx'=4,'tp'=4] {'ctx'}, dimensions={0}, use_global_device_ids=true | all-gather | bytes 327680 | tf_op jit(solution)/shard_map/all_gather | solution.py:106
  43.0 1.1 fusion.53
  44.1 6.9 %all-to-all-start.1 = ((f32[4,64,512]{2,1,0:T(8,128)}), f32[4,64,512]{2,1,0:T(8,128)S(1)}, u32[]{:S(2)}, u32[]{:S(2)}) async-start(f32[4,64,512]{2,1,0:T(8,128)} %bitcast.13), calls=%async_computation.1 | async-start | bytes 1048576 | tf_op jit(solution)/shard_map/all_to_all | solution.py:109
  51.1 9.3 %all-gather.1 = f32[8,64,12]{1,2,0:T(8,128)S(1)} all-gather(f32[1,64,12]{1,2,0:T(8,128)S(1)} %maximum_bitcast_fusion.1), channel_id=2, replica_groups=mesh['req'=2,'ctx'=4,'tp'=4] {'req','ctx'}, dimensions={0}, use_global_device_ids=true | all-gather | bytes 27648 | tf_op jit(solution)/shard_map/all_gather | solution.py:56
  60.3 0.6 fusion.52
  61.0 0.2 compare_reduce_fusion
  61.1 0.4 copy-done.5
  61.6 4.5 %all-to-all-done.1 = f32[4,64,512]{2,1,0:T(8,128)S(1)} async-done(((f32[4,64,512]{2,1,0:T(8,128)}), f32[4,64,512]{2,1,0:T(8,128)S(1)}, u32[]{:S(2)}, u32[]{:S(2)}) %all-to-all-start.1) | async-done | bytes 524320 | tf_op jit(solution)/shard_map/all_to_all | solution.py:109
  66.3 4.7 %collective-permute-start.2 = (bf16[64,512]{1,0:T(8,128)(2,1)S(1)}, bf16[64,512]{1,0:T(8,128)(2,1)S(1)}, u32[]{:S(2)}, u32[]{:S(2)}) collective-permute-start(bf16[64,512]{1,0:T(8,128)(2,1)S(1)} %get-tuple-element.8), channel_id=1, source_target_pairs={{0,19},{1,0},{2,1},{3,2},{16,3},{17,16},{18,17},{19,18},{4,23},{5,... | collective-permute-start | bytes 196616 | tf_op jit(solution)/shard_map/ppermute | solution.py:131
  71.0 0.2 fusion.13
  71.3 0.1 copy.61
  71.4 0.1 reshape.144
  71.6 1.7 collective-permute-done.1
  73.2 0.1 collective-permute-done.2
  73.3 5.3 %collective-permute-start.4 = (bf16[64,512]{1,0:T(8,128)(2,1)S(1)}, bf16[64,512]{1,0:T(8,128)(2,1)S(1)}, u32[]{:S(2)}, u32[]{:S(2)}) collective-permute-start(bf16[64,512]{1,0:T(8,128)(2,1)S(1)} %collective-permute-done.2), channel_id=1, source_target_pairs={{0,19},{1,0},{2,1},{3,2},{16,3},{17,16},{18,17},{19,18},{4,23},{5,... | collective-permute-start | bytes 196616 | tf_op jit(solution)/shard_map/ppermute | solution.py:131
  78.6 1.7 collective-permute-done.3
  80.3 0.2 collective-permute-done.4
  80.5 5.2 %collective-permute-start.6 = (bf16[64,512]{1,0:T(8,128)(2,1)S(1)}, bf16[64,512]{1,0:T(8,128)(2,1)S(1)}, u32[]{:S(2)}, u32[]{:S(2)}) collective-permute-start(bf16[64,512]{1,0:T(8,128)(2,1)S(1)} %collective-permute-done.4), channel_id=1, source_target_pairs={{0,19},{1,0},{2,1},{3,2},{16,3},{17,16},{18,17},{19,18},{4,23},{5,... | collective-permute-start | bytes 196616 | tf_op jit(solution)/shard_map/ppermute | solution.py:131
  85.8 1.5 collective-permute-done.5
  87.3 0.4 collective-permute-done.6
  87.6 6.6 %collective-permute-done.7 = bf16[64,512]{1,0:T(8,128)(2,1)S(1)} collective-permute-done((bf16[64,512]{1,0:T(8,128)(2,1)S(1)}, bf16[64,512]{1,0:T(8,128)(2,1)S(1)}, u32[]{:S(2)}, u32[]{:S(2)}) %collective-permute-start.7) | collective-permute-done | bytes 65568 | tf_op jit(solution)/shard_map/ppermute | solution.py:128
  94.2 1.3 fusion.6
  95.5 8.6 %convolution_convert_fusion.1 = bf16[32,64,352]{2,1,0:T(8,128)(2,1)} fusion(bf16[32,64,512]{2,1,0:T(8,128)(2,1)S(1)} %fusion.6, bf16[32,512,352]{1,2,0:T(8,128)(2,1)} %param.25), kind=kOutput, calls=%fused_computation.18 | convolution fusion | flops 738918400 | bytes 15073280 | tf_op jit(solution)/shard_map/esd,edf->esf/dot_general | solution.py:143
  104.1 2.5 %copy.62 = bf16[4,512,1,352]{1,3,2,0:T(8,128)(2,1)} copy(bf16[4,512,1,352]{3,1,0,2:T(8,128)(2,1)} %bitcast.77) | data formatting | bytes 2883584 | tf_op jit(solution)/shard_map/stack | solution.py:145
  106.7 8.6 %convolution_convert_fusion = bf16[32,64,352]{2,1,0:T(8,128)(2,1)} fusion(bf16[32,64,512]{2,1,0:T(8,128)(2,1)S(1)} %fusion.6, bf16[32,512,352]{1,2,0:T(8,128)(2,1)} %param.26), kind=kOutput, calls=%fused_computation.17 | convolution fusion | flops 738918400 | bytes 15073280 | tf_op jit(solution)/shard_map/esd,edf->esf/dot_general | solution.py:144
  115.3 1.7 copy.63
  117.0 3.2 %pad_maximum_fusion = bf16[4,512,2,352]{1,3,2,0:T(8,128)(2,1)} fusion(bf16[4,512,1,352]{1,3,2,0:T(8,128)(2,1)S(1)} %copy.63, bf16[4,512,1,352]{1,3,2,0:T(8,128)(2,1)} %copy.62), kind=kLoop, calls=%fused_computation.14 | loop fusion | flops 1441792 | bytes 5767168 | tf_op jit(solution)/shard_map/stack | solution.py:145
  120.2 5.3 %all-to-all-start.2 = ((bf16[4,512,2,352]{1,3,2,0:T(8,128)(2,1)}), bf16[4,512,2,352]{1,3,2,0:T(8,128)(2,1)S(1)}, u32[]{:S(2)}, u32[]{:S(2)}) async-start(bf16[4,512,2,352]{1,3,2,0:T(8,128)(2,1)} %pad_maximum_fusion), calls=%async_computation.2 | async-start | bytes 5767168 | tf_op jit(solution)/shard_map/all_to_all | solution.py:147
  125.5 0.2 fusion.14
  125.7 0.1 copy.67
  125.8 0.1 reshape.146
  125.9 0.7 dynamic-slice
  127.3 0.1 multiply_reduce_fusion
  127.4 33.4 %psum.7 = f32[64]{0:T(128)S(1)} all-reduce(f32[64]{0:T(128)S(1)} %multiply_reduce_fusion), channel_id=1, replica_groups=mesh['req'=2,'ctx'=4,'tp'=4] {'ctx'}, use_global_device_ids=true, to_apply=%region_9.10 | all-reduce | flops 64 | bytes 512 | tf_op jit(solution)/shard_map/psum | solution.py:114
  160.7 0.1 rsqrt_dynamic-update-slice_fusion
  160.8 17.4 %all-reduce = f32[512]{0:T(512)S(1)} all-reduce(f32[512]{0:T(512)S(1)} %rsqrt_dynamic-update-slice_fusion), channel_id=1, replica_groups=mesh['req'=2,'ctx'=4,'tp'=4] {'req','tp'}, use_global_device_ids=true, to_apply=%add | all-reduce | flops 512 | bytes 4096
  178.3 1.5 select_reduce_fusion
  179.8 0.1 reshape_broadcast_in_dim.3
  179.9 0.4 convert_reduce_fusion
  180.3 0.1 fusion.51
  180.4 0.3 copy.72
  180.7 0.3 copy.73
  181.0 1.0 fusion.16
  182.0 18.3 %all-gather.4.cloned.1.call-done = bf16[2048,352]{1,0:T(8,128)(2,1)} async-done(((bf16[512,352]{1,0:T(8,128)(2,1)}), bf16[2048,352]{1,0:T(8,128)(2,1)}) %all-gather.4.cloned.1.call-update) | async-done | bytes 1441808 | tf_op jit(solution)/shard_map/all_gather | solution.py:152
  200.3 8.2 %fusion.10 = bf16[512,512]{1,0:T(8,128)(2,1)S(1)} fusion(s32[32,512]{1,0:T(8,128)S(1)} %bitcast.86, bf16[32,64,352]{2,1,0:T(8,128)(2,1)} %bitcast.92, bf16[32,352,512]{2,1,0:T(8,128)(2,1)} %param.27, f32[32,64]{1,0:T(8,128)S(1)} %get-tuple-element.5), kind=kOutput, calls=%fused_computation.20 | convolution fusion | flops 1815347200 | bytes 13574144 | tf_op jit(solution)/shard_map/est,esd->td/dot_general | solution.py:155
  208.6 21.3 %all_to_all.20 = bf16[8,64,512]{2,1,0:T(8,128)(2,1)S(1)} all-to-all(bf16[8,64,512]{2,1,0:T(8,128)(2,1)S(1)} %bitcast.81), channel_id=1, replica_groups=mesh['req'=2,'ctx'=4,'tp'=4] {'req','tp'}, dimensions={0} | all-to-all | bytes 1048576 | tf_op jit(solution)/shard_map/all_to_all | solution.py:157
  230.0 2.8 %collective-permute-start.8 = (bf16[64,512]{1,0:T(8,128)(2,1)S(1)}, bf16[64,512]{1,0:T(8,128)(2,1)S(1)}, u32[]{:S(2)}, u32[]{:S(2)}) collective-permute-start(bf16[64,512]{1,0:T(8,128)(2,1)S(1)} %add_convert_fusion), channel_id=1, source_target_pairs={{0,0},{1,4},{2,8},{3,12},{4,1},{5,5},{6,9},{7,13},{8,2},{9,6},{10,... | collective-permute-start | bytes 196616 | tf_op jit(solution)/shard_map/ppermute | solution.py:159
  232.8 5.2 %collective-permute-done.8 = bf16[64,512]{1,0:T(8,128)(2,1)S(1)} collective-permute-done((bf16[64,512]{1,0:T(8,128)(2,1)S(1)}, bf16[64,512]{1,0:T(8,128)(2,1)S(1)}, u32[]{:S(2)}, u32[]{:S(2)}) %collective-permute-start.8) | collective-permute-done | bytes 65568 | tf_op jit(solution)/shard_map/ppermute | solution.py:159
  237.9 0.6 copy.91
  (69 shorter events, 0.6 us)
Async XLA Ops:
  6.5 36.5 %copy-start = (bf16[512,512]{1,0:T(8,128)(2,1)S(1)}, bf16[512,512]{1,0:T(8,128)(2,1)}, u32[]{:S(2)}) copy-start(bf16[512,512]{1,0:T(8,128)(2,1)} %param.21) | copy-start | bytes 1572868
  16.0 4.8 %copy-start.13 = (bf16[1,2048,1,128]{3,1,2,0:T(8,128)(2,1)S(1)}, bf16[1,2048,1,128]{3,1,2,0:T(8,128)(2,1)}, u32[]{:S(2)}) copy-start(bf16[1,2048,1,128]{3,1,2,0:T(8,128)(2,1)} %param.18) | copy-start | bytes 1572868
  16.0 4.8 %copy-start.14 = (bf16[256,1,128]{2,0,1:T(8,128)(2,1)S(1)}, bf16[256,1,128]{2,0,1:T(8,128)(2,1)}, u32[]{:S(2)}) copy-start(bf16[256,1,128]{2,0,1:T(8,128)(2,1)} %param.16) | copy-start | bytes 196612
  20.8 8.6 %copy-start.15 = (bf16[64,512]{1,0:T(8,128)(2,1)S(1)}, bf16[64,512]{1,0:T(8,128)(2,1)}, u32[]{:S(2)}) copy-start(bf16[64,512]{1,0:T(8,128)(2,1)} %param.20) | copy-start | bytes 196612
  20.8 13.1 %copy-start.11 = (s32[64,6]{0,1:T(8,128)S(1)}, s32[64,6]{0,1:T(8,128)}, u32[]{:S(2)}) copy-start(s32[64,6]{0,1:T(8,128)} %param.23) | copy-start | bytes 4612
  24.8 26.2 %copy-start.12 = (f32[64,6]{0,1:T(8,128)S(1)}, f32[64,6]{0,1:T(8,128)}, u32[]{:S(2)}) copy-start(f32[64,6]{0,1:T(8,128)} %param.24) | copy-start | bytes 4612
  25.9 10.9 %all-to-all-start = ((f32[4,136,256]{2,1,0:T(8,128)}), f32[4,136,256]{2,1,0:T(8,128)S(1)}, u32[]{:S(2)}, u32[]{:S(2)}) async-start(f32[4,136,256]{2,1,0:T(8,128)} %maximum_bitcast_fusion), calls=%async_computation | async-start | bytes 1114112 | tf_op jit(solution)/shard_map/all_to_all | solution.py:104
  29.4 36.8 %collective-permute-start = (bf16[64,512]{1,0:T(8,128)(2,1)S(1)}, bf16[64,512]{1,0:T(8,128)(2,1)S(1)}, u32[]{:S(2)}, u32[]{:S(2)}) collective-permute-start(bf16[64,512]{1,0:T(8,128)(2,1)S(1)} %copy-done.15), channel_id=1, source_target_pairs={{0,0},{1,4},{2,8},{3,12},{4,1},{5,5},{6,9},{7,13},{8,2},{9,6},{10,... | collective-permute-start | bytes 196616 | tf_op jit(solution)/shard_map/ppermute | solution.py:102
  44.1 21.9 %all-to-all-start.1 = ((f32[4,64,512]{2,1,0:T(8,128)}), f32[4,64,512]{2,1,0:T(8,128)S(1)}, u32[]{:S(2)}, u32[]{:S(2)}) async-start(f32[4,64,512]{2,1,0:T(8,128)} %bitcast.13), calls=%async_computation.1 | async-start | bytes 1048576 | tf_op jit(solution)/shard_map/all_to_all | solution.py:109
  61.0 0.6 copy-start.5
  66.1 28.1 %copy-start.2 = (bf16[64,512]{1,0:T(8,128)(2,1)}, bf16[64,512]{1,0:T(8,128)(2,1)S(1)}, u32[]{:S(2)}) copy-start(bf16[64,512]{1,0:T(8,128)(2,1)S(1)} %collective-permute-done) | copy-start | bytes 196612
  66.2 7.0 %collective-permute-start.1 = (bf16[64,512]{1,0:T(8,128)(2,1)S(1)}, bf16[64,512]{1,0:T(8,128)(2,1)S(1)}, u32[]{:S(2)}, u32[]{:S(2)}) collective-permute-start(bf16[64,512]{1,0:T(8,128)(2,1)S(1)} %get-tuple-element.8), channel_id=1, source_target_pairs={{0,1},{1,2},{2,3},{3,16},{16,17},{17,18},{18,19},{19,0},{4,5},{5,6... | collective-permute-start | bytes 196616 | tf_op jit(solution)/shard_map/ppermute | solution.py:128
  66.3 7.0 %collective-permute-start.2 = (bf16[64,512]{1,0:T(8,128)(2,1)S(1)}, bf16[64,512]{1,0:T(8,128)(2,1)S(1)}, u32[]{:S(2)}, u32[]{:S(2)}) collective-permute-start(bf16[64,512]{1,0:T(8,128)(2,1)S(1)} %get-tuple-element.8), channel_id=1, source_target_pairs={{0,19},{1,0},{2,1},{3,2},{16,3},{17,16},{18,17},{19,18},{4,23},{5,... | collective-permute-start | bytes 196616 | tf_op jit(solution)/shard_map/ppermute | solution.py:131
  71.5 32.6 %copy-start.7 = (s32[512,32]{0,1:T(8,128)}, s32[512,32]{0,1:T(8,128)S(1)}, u32[]{:S(2)}) copy-start(s32[512,32]{0,1:T(8,128)S(1)} %reshape.144) | copy-start | bytes 196612
  73.2 7.1 %collective-permute-start.3 = (bf16[64,512]{1,0:T(8,128)(2,1)S(1)}, bf16[64,512]{1,0:T(8,128)(2,1)S(1)}, u32[]{:S(2)}, u32[]{:S(2)}) collective-permute-start(bf16[64,512]{1,0:T(8,128)(2,1)S(1)} %collective-permute-done.1), channel_id=1, source_target_pairs={{0,1},{1,2},{2,3},{3,16},{16,17},{17,18},{18,19},{19,0},{4,5},{5,6... | collective-permute-start | bytes 196616 | tf_op jit(solution)/shard_map/ppermute | solution.py:128
  73.3 7.2 %collective-permute-start.4 = (bf16[64,512]{1,0:T(8,128)(2,1)S(1)}, bf16[64,512]{1,0:T(8,128)(2,1)S(1)}, u32[]{:S(2)}, u32[]{:S(2)}) collective-permute-start(bf16[64,512]{1,0:T(8,128)(2,1)S(1)} %collective-permute-done.2), channel_id=1, source_target_pairs={{0,19},{1,0},{2,1},{3,2},{16,3},{17,16},{18,17},{19,18},{4,23},{5,... | collective-permute-start | bytes 196616 | tf_op jit(solution)/shard_map/ppermute | solution.py:131
  80.3 7.0 %collective-permute-start.5 = (bf16[64,512]{1,0:T(8,128)(2,1)S(1)}, bf16[64,512]{1,0:T(8,128)(2,1)S(1)}, u32[]{:S(2)}, u32[]{:S(2)}) collective-permute-start(bf16[64,512]{1,0:T(8,128)(2,1)S(1)} %collective-permute-done.3), channel_id=1, source_target_pairs={{0,1},{1,2},{2,3},{3,16},{16,17},{17,18},{18,19},{19,0},{4,5},{5,6... | collective-permute-start | bytes 196616 | tf_op jit(solution)/shard_map/ppermute | solution.py:128
  80.5 7.1 %collective-permute-start.6 = (bf16[64,512]{1,0:T(8,128)(2,1)S(1)}, bf16[64,512]{1,0:T(8,128)(2,1)S(1)}, u32[]{:S(2)}, u32[]{:S(2)}) collective-permute-start(bf16[64,512]{1,0:T(8,128)(2,1)S(1)} %collective-permute-done.4), channel_id=1, source_target_pairs={{0,19},{1,0},{2,1},{3,2},{16,3},{17,16},{18,17},{19,18},{4,23},{5,... | collective-permute-start | bytes 196616 | tf_op jit(solution)/shard_map/ppermute | solution.py:131
  87.3 7.0 %collective-permute-start.7 = (bf16[64,512]{1,0:T(8,128)(2,1)S(1)}, bf16[64,512]{1,0:T(8,128)(2,1)S(1)}, u32[]{:S(2)}, u32[]{:S(2)}) collective-permute-start(bf16[64,512]{1,0:T(8,128)(2,1)S(1)} %collective-permute-done.5), channel_id=1, source_target_pairs={{0,1},{1,2},{2,3},{3,16},{16,17},{17,18},{18,19},{19,0},{4,5},{5,6... | collective-permute-start | bytes 196616 | tf_op jit(solution)/shard_map/ppermute | solution.py:128
  120.2 5.4 %copy-start.6 = (s32[8,64,6]{1,2,0:T(8,128)S(1)}, s32[8,64,6]{1,2,0:T(8,128)}, u32[]{:S(2)}) copy-start(s32[8,64,6]{1,2,0:T(8,128)} %copy-done.5) | copy-start | bytes 36868
  120.2 5.4 %copy-start.10 = (f32[8,64,6]{1,2,0:T(8,128)S(1)}, f32[8,64,6]{1,2,0:T(8,128)}, u32[]{:S(2)}) copy-start(f32[8,64,6]{1,2,0:T(8,128)} %get-tuple-element.13) | copy-start | bytes 36868
  120.2 5.7 %copy-start.16 = (u32[32]{0:T(128)S(1)}, u32[32]{0:T(128)}, u32[]{:S(2)}) copy-start(u32[32]{0:T(128)} %constant.145) | copy-start | bytes 388
  120.2 7.0 %copy-start.3 = (bf16[64,512]{1,0:T(8,128)(2,1)S(1)}, bf16[64,512]{1,0:T(8,128)(2,1)}, u32[]{:S(2)}) copy-start(bf16[64,512]{1,0:T(8,128)(2,1)} %copy-done.2) | copy-start | bytes 196612
  120.2 58.1 %copy-start.8 = (s32[512,32]{0,1:T(8,128)S(1)}, s32[512,32]{0,1:T(8,128)}, u32[]{:S(2)}) copy-start(s32[512,32]{0,1:T(8,128)} %copy-done.7) | copy-start | bytes 196612
  120.2 59.6 %all-to-all-start.2 = ((bf16[4,512,2,352]{1,3,2,0:T(8,128)(2,1)}), bf16[4,512,2,352]{1,3,2,0:T(8,128)(2,1)S(1)}, u32[]{:S(2)}, u32[]{:S(2)}) async-start(bf16[4,512,2,352]{1,3,2,0:T(8,128)(2,1)} %pad_maximum_fusion), calls=%async_computation.2 | async-start | bytes 5767168 | tf_op jit(solution)/shard_map/all_to_all | solution.py:147
  125.5 74.8 %all-gather.4.cloned.1.call-start = ((), (), s32[]{:S(2)}) async-start(), calls=%async_computation.4 | async-start | bytes 1966080 | tf_op jit(solution)/shard_map/all_gather | solution.py:152
  180.3 20.0 %copy-start.9 = (s32[512,32]{0,1:T(8,128)S(1)}, s32[512,32]{0,1:T(8,128)}, u32[]{:S(2)}) copy-start(s32[512,32]{0,1:T(8,128)} %copy-done.7) | copy-start | bytes 196612
  200.3 29.6 %copy-start.4 = (bf16[64,512]{1,0:T(8,128)(2,1)S(1)}, bf16[64,512]{1,0:T(8,128)(2,1)}, u32[]{:S(2)}) copy-start(bf16[64,512]{1,0:T(8,128)(2,1)} %copy-done.2) | copy-start | bytes 196612
  200.3 38.3 %copy-start.1 = (bf16[512,512]{1,0:T(8,128)(2,1)S(1)}, bf16[512,512]{1,0:T(8,128)(2,1)}, u32[]{:S(2)}) copy-start(bf16[512,512]{1,0:T(8,128)(2,1)} %param.21) | copy-start | bytes 1572868
  230.0 8.0 %collective-permute-start.8 = (bf16[64,512]{1,0:T(8,128)(2,1)S(1)}, bf16[64,512]{1,0:T(8,128)(2,1)S(1)}, u32[]{:S(2)}, u32[]{:S(2)}) collective-permute-start(bf16[64,512]{1,0:T(8,128)(2,1)S(1)} %add_convert_fusion), channel_id=1, source_target_pairs={{0,0},{1,4},{2,8},{3,12},{4,1},{5,5},{6,9},{7,13},{8,2},{9,6},{10,... | collective-permute-start | bytes 196616 | tf_op jit(solution)/shard_map/ppermute | solution.py:159
Sparse Core Ops, SparseCore 0:
  182.2 18.1 all-gather.3
